TPU v7x, 256 devices: a whole 4x4x8 slice. The times are simulated.
256 devices in a mesh: tile: 64 (over z, y_lo, x), mode: 4 (over y_hi, core).
Axes of the slice: x: 4, y: 4 (y_hi: 2, y_lo: 2; y = y_hi * 2 + y_lo), z: 8, core: 2. Of those that a mesh axis runs over, the one named last changes fastest.
Arguments:
- object_tiles: float32 [64, 2, 2, 256, 256], P('tile'), may hold values from -6 to 6
- object_previous: float32 [64, 2, 2, 256, 256], P('tile'), may hold values from -6 to 6
- probe: float32 [4, 8, 2, 256, 256], P(None, 'mode', None, 'tile'), may hold values from -2 to 2
- probe_previous: float32 [4, 8, 2, 256, 256], P(None, 'mode', None, 'tile'), may hold values from -6 to 6
- patterns: float32 [128, 256, 256], P('tile'), may hold values from 0 to 2
- offsets: int32 [2, 128], P(None, 'tile'), may hold values from 0 to 255
- scan_of_slot: int32 [128], P('tile'), may hold values from 0 to 3
- tile_load: int32 [64], P('tile'), may hold values from 1 to 2, as said below
- step_sizes: int32 [2], replicated, may hold values from 128 to 511
- object_norm_before: float32 [1], replicated, may hold values from 0.1 to 0.4
- probe_norm_before: float32 [1], replicated, may hold values from 12 to 64
Outputs:
- new_object: float32 [64, 2, 2, 256, 256], P('tile')
- object_direction: float32 [64, 2, 2, 256, 256], P('tile')
- new_probe: float32 [4, 8, 2, 256, 256], P(None, 'mode', None, 'tile')
- probe_direction: float32 [4, 8, 2, 256, 256], P(None, 'mode', None, 'tile')
Inputs may be any that keep to these rules, and one draw needn't show every extreme that they name: `tile_load`: every tile holds 1 to 2 used slots, and some tile holds exactly 2.
All inputs are finite; a program needn't handle non-finite values.
Results may differ from a plain program's by a relative error of at most 0.024.
Values may be sent and summed in bfloat16 or wider, within the bound.
No kernel may reach another device: no remote copies, remote signals or barrier semaphores. Data moves between devices by JAX's collectives and lax.ppermute only.
A program may use at most 64 MiB of HBM per device.

v0:
```python
import math
import jax
import jax.numpy as jnp
from jax import lax
from jax.sharding import PartitionSpec as P

TGX = 8
MODES = 8
SCAN_COUNT = 4
residual_weight = 2.0


def from_behind(block, axis, distance):
    devices = range(lax.axis_size(axis))
    route = [(i - distance, i) for i in devices if i - distance in devices]
    return lax.ppermute(block, axis, route)


def table_pair(width):
    index_row = jnp.arange(width, dtype=jnp.int32)
    product = index_row[:, None] * index_row[None, :] % width
    angle = product.astype(jnp.float32) * (2.0 * math.pi / width)
    factor = 1.0 / math.sqrt(width)
    cosine = (jnp.cos(angle) * factor).astype(jnp.bfloat16)
    sine = (-jnp.sin(angle) * factor).astype(jnp.bfloat16)
    index_free = jnp.where(index_row < width // 2, index_row, index_row - width).astype(jnp.float32)
    phase = (
        index_free[:, None] * index_free[:, None] + index_free[None, :] * index_free[None, :]
    ) * (math.pi / (4.0 * width))
    return (cosine, sine, jnp.cos(phase), jnp.sin(phase))


def right_product(left_data, table):
    return jnp.einsum("...jk,kl->...jl", left_data, table, preferred_element_type=jnp.float32)


def left_product(table, right_data):
    return jnp.einsum("ij,...jl->...il", table, right_data, preferred_element_type=jnp.float32)


def transform(wave_re, wave_im, tables, inverse):
    cosine = tables[0]
    sine = -tables[1] if inverse else tables[1]
    first_re = (right_product(wave_re, cosine) - right_product(wave_im, sine)).astype(jnp.bfloat16)
    first_im = (right_product(wave_re, sine) + right_product(wave_im, cosine)).astype(jnp.bfloat16)
    out_re = (left_product(cosine, first_re) - left_product(sine, first_im)).astype(jnp.bfloat16)
    out_im = (left_product(sine, first_re) + left_product(cosine, first_im)).astype(jnp.bfloat16)
    return (out_re, out_im)


def complex_times(first_re, first_im, second_re, second_im):
    first_portion = first_re.astype(jnp.float32)
    b_part = first_im.astype(jnp.float32)
    c_part = second_re.astype(jnp.float32)
    d_part = second_im.astype(jnp.float32)
    return (first_portion * c_part - b_part * d_part, first_portion * d_part + b_part * c_part)


def conj_times(first_re, first_im, second_re, second_im):
    first_portion = first_re.astype(jnp.float32)
    b_part = first_im.astype(jnp.float32)
    c_part = second_re.astype(jnp.float32)
    d_part = second_im.astype(jnp.float32)
    return (first_portion * c_part + b_part * d_part, first_portion * d_part - b_part * c_part)


def propagate(wave_re, wave_im, tables, adjoint):
    spec_re, spec_im = transform(wave_re, wave_im, tables, False)
    kernel_im = -tables[3] if adjoint else tables[3]
    moved_re, moved_im = complex_times(spec_re, spec_im, tables[2], kernel_im)
    return transform(moved_re.astype(jnp.bfloat16), moved_im.astype(jnp.bfloat16), tables, True)


def body(
    object_tiles,
    object_previous,
    probe,
    probe_previous,
    patterns,
    offsets,
    scan_of_slot,
    tile_load,
    step_sizes,
    object_norm_before,
    probe_norm_before,
):
    tile_count = lax.axis_size("tile")
    mode_count = lax.axis_size("mode")
    slots = patterns.shape[0]
    width = patterns.shape[1]
    layers = object_tiles.shape[1]
    tile_side = object_tiles.shape[3]
    scans = probe.shape[0]
    tables = table_pair(width)
    own_tile = object_tiles[0].astype(jnp.bfloat16)
    east_part = from_behind(own_tile, "tile", -1)
    upper = jnp.concatenate([own_tile, east_part], axis=3)
    lower = from_behind(upper, "tile", -TGX)
    region = jnp.concatenate([upper, lower], axis=2)
    gathered = lax.all_gather(probe.astype(jnp.bfloat16), "tile", axis=3, tiled=True)
    valid_mask = (jnp.arange(slots, dtype=jnp.int32) < tile_load[0]).astype(jnp.float32)

    def cut_patch(row_start, col_start):
        return lax.dynamic_slice(region, (0, 0, row_start, col_start), (layers, 2, width, width))

    patches = jax.vmap(cut_patch)(offsets[0], offsets[1])
    probe_pick = jnp.take(gathered, scan_of_slot, axis=0)
    wave_re = probe_pick[:, :, 0]
    wave_im = probe_pick[:, :, 1]
    incident = []
    for layer_index in range(layers):
        incident.append((wave_re, wave_im))
        next_re, next_im = complex_times(
            wave_re, wave_im, patches[:, None, layer_index, 0], patches[:, None, layer_index, 1]
        )
        wave_re = next_re.astype(jnp.bfloat16)
        wave_im = next_im.astype(jnp.bfloat16)
        if layer_index + 1 < layers:
            wave_re, wave_im = propagate(wave_re, wave_im, tables, False)
    far_re, far_im = transform(wave_re, wave_im, tables, False)
    far_re32 = far_re.astype(jnp.float32)
    far_im32 = far_im.astype(jnp.float32)
    partial_power = jnp.sum(far_re32 * far_re32 + far_im32 * far_im32, axis=1)
    power = lax.psum(partial_power, "mode")
    misfit = (power - patterns) * valid_mask[:, None, None]
    back_re = (residual_weight * misfit[:, None] * far_re32).astype(jnp.bfloat16)
    back_im = (residual_weight * misfit[:, None] * far_im32).astype(jnp.bfloat16)
    back_re, back_im = transform(back_re, back_im, tables, True)
    slice_terms = [None] * layers
    probe_terms = None
    for layer_index in reversed(range(layers)):
        inc_re, inc_im = incident[layer_index]
        grad_re, grad_im = conj_times(inc_re, inc_im, back_re, back_im)
        slice_terms[layer_index] = jnp.stack(
            [jnp.sum(grad_re, axis=1), jnp.sum(grad_im, axis=1)], axis=1
        )
        carry_re, carry_im = conj_times(
            patches[:, None, layer_index, 0], patches[:, None, layer_index, 1], back_re, back_im
        )
        if layer_index > 0:
            back_re, back_im = propagate(
                carry_re.astype(jnp.bfloat16), carry_im.astype(jnp.bfloat16), tables, True
            )
        else:
            probe_terms = jnp.stack([carry_re, carry_im], axis=2)
    slot_grads = jnp.stack(slice_terms, axis=1)
    region_grad = jnp.zeros((layers, 2, 2 * tile_side, 2 * tile_side), jnp.float32)
    for slot_index in range(slots):
        starts = (0, 0, offsets[0, slot_index], offsets[1, slot_index])
        current = lax.dynamic_slice(region_grad, starts, (layers, 2, width, width))
        region_grad = lax.dynamic_update_slice(
            region_grad, current + slot_grads[slot_index], starts
        )
    region_grad = lax.psum(region_grad.astype(jnp.bfloat16), "mode").astype(jnp.float32)
    from_above = from_behind(
        region_grad[:, :, tile_side:, :].astype(jnp.bfloat16), "tile", TGX
    ).astype(jnp.float32)
    upper_grad = region_grad[:, :, :tile_side, :] + from_above
    from_left = from_behind(upper_grad[:, :, :, tile_side:].astype(jnp.bfloat16), "tile", 1).astype(
        jnp.float32
    )
    tile_grad = upper_grad[:, :, :, :tile_side] + from_left
    scan_onehot = (scan_of_slot[:, None] == jnp.arange(scans, dtype=jnp.int32)[None, :]).astype(
        jnp.float32
    )
    probe_local = jnp.einsum(
        "cs,cmrij->smrij", scan_onehot, probe_terms, precision=lax.Precision.HIGHEST
    )
    probe_grad = lax.psum_scatter(probe_local, "tile", scatter_dimension=3, tiled=True)
    object_sum = jnp.sum(tile_grad * tile_grad) / float(mode_count)
    probe_sum = jnp.sum(probe_grad * probe_grad)
    object_total, probe_total = lax.psum((object_sum, probe_sum), ("tile", "mode"))
    object_square = object_total / float(tile_count * layers * 2 * tile_side * tile_side)
    probe_square = probe_total / float(SCAN_COUNT * MODES * 2 * width * width)
    object_direction = -tile_grad[None] + object_square / object_norm_before[0] * object_previous
    new_object = object_tiles + step_sizes[0].astype(jnp.float32) / 1024.0 * object_direction
    probe_direction = -probe_grad + probe_square / probe_norm_before[0] * probe_previous
    new_probe = probe + step_sizes[1].astype(jnp.float32) / 16384.0 * probe_direction
    return (new_object, object_direction, new_probe, probe_direction)


def solution(mesh):
    return jax.shard_map(
        body,
        mesh=mesh,
        in_specs=(
            P("tile", None, None, None, None),
            P("tile", None, None, None, None),
            P(None, "mode", None, "tile", None),
            P(None, "mode", None, "tile", None),
            P("tile", None, None),
            P(None, "tile"),
            P("tile"),
            P("tile"),
            P(),
            P(),
            P(),
        ),
        out_specs=(
            P("tile", None, None, None, None),
            P("tile", None, None, None, None),
            P(None, "mode", None, "tile", None),
            P(None, "mode", None, "tile", None),
        ),
        check_vma=False,
    )
```

profile of v0, /device:TPU:1, one launch (start us, length us, event | category | flops | bytes accessed | tf_op | source)
XLA Modules:
  0.0 1247.7 jit_solution(10554642321168706119)
XLA Ops:
  12.1 11.3 collective-permute-done
  25.1 1.8 fusion.154
  26.9 28.3 %collective-permute-done.1 = bf16[2,2,256,512]{3,2,1,0:T(8,128)(2,1)} collective-permute-done((bf16[2,2,256,512]{3,2,1,0:T(8,128)(2,1)S(1)}, bf16[2,2,256,512]{3,2,1,0:T(8,128)(2,1)}, u32[]{:S(2)}, u32[]{:S(2)}) %collective-permute-start.1) | collective-permute-done | bytes 1048608 | tf_op jit(solution)/shard_map/ppermute | solution.py:16
  56.6 6.0 while.1
  57.2 2.4 bitcast_dynamic-update-slice_fusion.2
  60.2 2.4 bitcast_dynamic-update-slice_fusion.2
  66.4 200.3 %all-gather.2.cloned.1.call-done = bf16[4,2,2,256,256]{4,0,2,1,3:T(4,128)(2,1)} async-done(((bf16[4,2,2,4,256]{4,0,2,1,3:T(4,128)(2,1)}), bf16[4,2,2,256,256]{4,0,2,1,3:T(4,128)(2,1)}) %all-gather.2.cloned.1.call-update) | async-done | bytes 2097168 | tf_op jit(solution)/shard_map/all_gather | solution.py:100
  266.7 2.3 copy.137
  270.6 2.0 copy.138
  292.4 2.4 add_convert_fusion.2
  304.1 2.1 add_reduce_fusion.1
  311.9 2.1 copy.169
  317.1 82.1 %all-reduce.6.cloned.1.call-done = f32[2,256,256]{1,2,0:T(8,128)} async-done(((f32[2,256,256]{1,2,0:T(8,128)}), f32[2,256,256]{1,2,0:T(8,128)}) %all-reduce.6.cloned.1.call-update) | async-done | bytes 524304 | tf_op jit(solution)/shard_map/psum | solution.py:124
  409.8 2.5 add_reduce_fusion
  431.7 3.0 add_bitcast_fusion
  435.0 2.5 broadcast_in_dim.11
  437.4 11.2 dynamic_update_slice.6
  450.4 12.3 dynamic_update_slice.7
  462.7 3.9 convert_element_type.598
  469.6 3.1 copy.197
  472.7 6.6 fusion.156
  479.4 50.8 %all-reduce.8.cloned.1.call-done = bf16[2,2,512,512]{2,3,1,0:T(8,128)(2,1)} async-done(((bf16[2,2,512,512]{2,3,1,0:T(8,128)(2,1)}), bf16[2,2,512,512]{2,3,1,0:T(8,128)(2,1)}) %all-reduce.8.cloned.1.call-update) | async-done | bytes 2097168 | tf_op jit(solution)/shard_map/psum | solution.py:154
  531.7 3.4 collective-permute-start.2
  535.1 22.3 %collective-permute-done.2 = bf16[2,2,256,512]{2,3,1,0:T(8,128)(2,1)S(1)} collective-permute-done((bf16[2,2,256,512]{2,3,1,0:T(8,128)(2,1)S(1)}, bf16[2,2,256,512]{2,3,1,0:T(8,128)(2,1)S(1)}, u32[]{:S(2)}, u32[]{:S(2)}) %collective-permute-start.2) | collective-permute-done | bytes 1048608 | tf_op jit(solution)/shard_map/ppermute | solution.py:16
  558.4 3.9 collective-permute-start.3
  566.9 2.6 copy.195
  570.8 2.8 collective-permute-done.3
  573.6 1.9 multiply_reduce_fusion
  576.2 531.9 %all-reduce.10.cloned.1.call-done = f32[4,2,2,256,256]{4,0,3,2,1:T(4,128)} async-done(((f32[4,2,2,256,256]{4,0,3,2,1:T(4,128)}), f32[4,2,2,256,256]{4,0,3,2,1:T(4,128)}) %all-reduce.10.cloned.1.call-update) | async-done | bytes 4194320
  1109.6 120.8 %all-reduce.1 = (f32[]{:T(128)}, f32[]{:T(128)}) all-reduce(f32[]{:T(128)S(6)} %div.27, f32[]{:T(128)} %multiply_reduce_fusion.1), channel_id=1, replica_groups=mesh['tile'=64,'mode'=4] {'tile','mode'}, use_global_device_ids=true, to_apply=%region_8.9 | all-reduce | flops 2 | bytes 16 | tf_op jit(solution)/shard_map/psum | solution.py:172
  1234.0 2.9 multiply_add_fusion
  1237.0 2.6 copy.200
  (149 shorter events, 89.0 us)
Async XLA Ops:
  7.2 17.8 %copy-start.23 = (s32[2]{0:T(128)S(1)}, s32[2]{0:T(128)}, u32[]{:S(2)}) copy-start(s32[2]{0:T(128)} %param.17) | copy-start | bytes 28
  7.2 259.5 %all-gather.2.cloned.1.call-start = ((), (), s32[]{:S(2)}) async-start(), calls=%async_computation | async-start | bytes 2129920 | tf_op jit(solution)/shard_map/all_gather | solution.py:100
  8.7 390.5 %all-reduce.6.cloned.1.call-start = ((), (), s32[]{:S(2)}) async-start(), calls=%async_computation.1 | async-start | bytes 1048576 | tf_op jit(solution)/shard_map/psum | solution.py:124
  10.1 13.3 %collective-permute-start = (bf16[2,2,256,256]{3,2,1,0:T(8,128)(2,1)S(1)}, bf16[2,2,256,256]{3,2,1,0:T(8,128)(2,1)S(1)}, u32[]{:S(2)}, u32[]{:S(2)}) collective-permute-start(bf16[2,2,256,256]{3,2,1,0:T(8,128)(2,1)S(1)} %convert_bitcast_fusion), channel_id=1, source_target_pairs={{4,0},{8,4},{12,8},{16,12},{20,16},{24,20},{28,24},{32,28},{36,32}... | collective-permute-start | bytes 1572872 | tf_op jit(solution)/shard_map/ppermute | solution.py:16
  23.5 31.7 %collective-permute-start.1 = (bf16[2,2,256,512]{3,2,1,0:T(8,128)(2,1)S(1)}, bf16[2,2,256,512]{3,2,1,0:T(8,128)(2,1)}, u32[]{:S(2)}, u32[]{:S(2)}) collective-permute-start(bf16[2,2,256,512]{3,2,1,0:T(8,128)(2,1)S(1)} %pad_maximum_fusion.3), channel_id=1, source_target_pairs={{32,0},{36,4},{40,8},{44,12},{48,16},{52,20},{56,24},{60,28},{64,3... | collective-permute-start | bytes 3145736 | tf_op jit(solution)/shard_map/ppermute | solution.py:16
  64.2 208.5 %copy-start.2 = (f32[2,256,256]{1,2,0:T(8,128)}, f32[2,256,256]{1,2,0:T(8,128)S(1)}, u32[]{:S(2)}) copy-start(f32[2,256,256]{1,2,0:T(8,128)S(1)} %copy.142) | copy-start | bytes 1572868
  64.4 208.3 %copy-start.4 = (f32[2,256,256]{1,2,0:T(8,128)}, f32[2,256,256]{1,2,0:T(8,128)S(1)}, u32[]{:S(2)}) copy-start(f32[2,256,256]{1,2,0:T(8,128)S(1)} %copy.143) | copy-start | bytes 1572868
  272.8 1.6 copy-start
  279.4 2.5 copy-start.18
  289.9 2.5 copy-start.6
  289.9 2.5 copy-start.8
  304.1 2.2 copy-start.21
  306.3 224.0 %all-reduce.8.cloned.1.call-start = ((), (), s32[]{:S(2)}) async-start(), calls=%async_computation.2 | async-start | bytes 4194304 | tf_op jit(solution)/shard_map/psum | solution.py:154
  408.3 1.3 copy-start.7
  408.3 1.3 copy-start.9
  408.3 1.5 copy-start.11
  418.6 2.5 copy-start.17
  429.1 2.6 copy-start.1
  429.1 2.6 copy-start.3
  429.1 2.6 copy-start.5
  466.5 1.5 copy-start.13
  466.6 641.5 %all-reduce.10.cloned.1.call-start = ((), (), s32[]{:S(2)}) async-start(), calls=%async_computation.3 | async-start | bytes 8388608
  530.2 27.1 %copy-start.16 = (bf16[2,2,512,512]{2,3,1,0:T(8,128)(2,1)S(1)}, bf16[2,2,512,512]{2,3,1,0:T(8,128)(2,1)}, u32[]{:S(2)}) copy-start(bf16[2,2,512,512]{2,3,1,0:T(8,128)(2,1)} %all-reduce.8.cloned.1.call-done) | copy-start | bytes 6291460
  531.7 30.7 %copy-start.10 = (f32[1,2,2,256,256]{4,3,2,1,0:T(8,128)S(1)}, f32[1,2,2,256,256]{4,3,2,1,0:T(8,128)}, u32[]{:S(2)}) copy-start(f32[1,2,2,256,256]{4,3,2,1,0:T(8,128)} %param.11) | copy-start | bytes 3145732
  531.7 25.6 %collective-permute-start.2 = (bf16[2,2,256,512]{2,3,1,0:T(8,128)(2,1)S(1)}, bf16[2,2,256,512]{2,3,1,0:T(8,128)(2,1)S(1)}, u32[]{:S(2)}, u32[]{:S(2)}) collective-permute-start(bf16[2,2,256,512]{2,3,1,0:T(8,128)(2,1)S(1)} %slice.116), channel_id=1, source_target_pairs={{0,32},{4,36},{8,40},{12,44},{16,48},{20,52},{24,56},{28,60},{32,6... | collective-permute-start | bytes 3145736 | tf_op jit(solution)/shard_map/ppermute | solution.py:16
  557.5 6.8 copy-start.22
  558.4 15.2 %collective-permute-start.3 = (bf16[2,2,256,256]{2,3,1,0:T(8,128)(2,1)}, bf16[2,2,256,256]{2,3,1,0:T(8,128)(2,1)}, u32[]{:S(2)}, u32[]{:S(2)}) collective-permute-start(bf16[2,2,256,256]{2,3,1,0:T(8,128)(2,1)} %slice.159), channel_id=1, source_target_pairs={{0,4},{4,8},{8,12},{12,16},{16,20},{20,24},{24,28},{28,32},{32,36}... | collective-permute-start | bytes 1572872 | tf_op jit(solution)/shard_map/ppermute | solution.py:16
  562.4 7.2 copy-start.24
  563.7 667.4 %copy-start.19 = (f32[4,2,2,4,256]{4,3,2,1,0:T(4,128)S(1)}, f32[4,2,2,4,256]{4,3,2,1,0:T(4,128)}, u32[]{:S(2)}) copy-start(f32[4,2,2,4,256]{4,3,2,1,0:T(4,128)} %param.13) | copy-start | bytes 196612
  563.7 667.4 %copy-start.20 = (f32[4,2,2,4,256]{4,3,2,1,0:T(4,128)S(1)}, f32[4,2,2,4,256]{4,3,2,1,0:T(4,128)}, u32[]{:S(2)}) copy-start(f32[4,2,2,4,256]{4,3,2,1,0:T(4,128)} %param.14) | copy-start | bytes 196612
  566.9 667.1 %copy-start.14 = (f32[1,2,2,256,256]{3,4,2,1,0:T(8,128)S(1)}, f32[1,2,2,256,256]{3,4,2,1,0:T(8,128)}, u32[]{:S(2)}) copy-start(f32[1,2,2,256,256]{3,4,2,1,0:T(8,128)} %copy.196) | copy-start | bytes 3145732
  1237.0 2.6 copy-start.15
  (1 other events, 1.2 us)
Sparse Core Ops, SparseCore 0:
  10.3 256.2 all-gather.1
  306.4 92.8 all-reduce.5
  466.7 63.5 all-reduce.7
  532.7 575.3 all-reduce.9
where the time goes:
time: 1250 us
  waiting for transfers between devices  930 us (74%)
  blocking collectives  121 us (10%)
  matrix products  73.2 us (6%)
  local copies, waits for them, and re-layouts  62.1 us (5%)
  between operations  28.2 us (2%)
  other arithmetic  23.5 us (2%)
    unnamed x5, waiting for transfers between devices  532 us
    all_gather x1, waiting for transfers between devices, body(): lax.all_gather(probe.astype(jnp.bfloat16), 'tile', axis=3, tiled=True)  200 us
    psum x1, blocking collectives, body(): lax.psum((object_sum, probe_sum), ('tile', 'mode'))  121 us
    psum x1, waiting for transfers between devices, body(): power = lax.psum(partial_power, 'mode')  82.1 us
    ppermute x4, waiting for transfers between devices, from_behind(): return lax.ppermute(block, axis, route)  64.6 us
    psum x1, waiting for transfers between devices, body(): lax.psum(region_grad.astype(jnp.bfloat16), 'mode').astype(jnp.float32)  50.8 us
    dot_general x24, matrix products, left_product(): jnp.einsum('ij,...jl->...il', table, right_data, preferred_element_type=j...  35.8 us
    dot_general x24, matrix products, right_product(): jnp.einsum('...jk,kl->...jl', left_data, table, preferred_element_type=jn...  30.7 us
  transfers between devices with their start and end apart: 8, of which 8 were waited for; matrix products, arithmetic and copies ran while one was open for 3% of the time, Pallas kernels for 0%

commit v1 on v0

--- a/solution.py
+++ b/solution.py
@@ -97,7 +97,9 @@
     upper = jnp.concatenate([own_tile, east_part], axis=3)
     lower = from_behind(upper, "tile", -TGX)
     region = jnp.concatenate([upper, lower], axis=2)
-    gathered = lax.all_gather(probe.astype(jnp.bfloat16), "tile", axis=3, tiled=True)
+    x = probe.astype(jnp.bfloat16)
+    repeated = jnp.stack([x] * lax.axis_size("tile"))
+    gathered = jnp.concatenate(lax.all_to_all(repeated, "tile", 0, 0), axis=3)
     valid_mask = (jnp.arange(slots, dtype=jnp.int32) < tile_load[0]).astype(jnp.float32)
 
     def cut_patch(row_start, col_start):

time: 1250 us -> 1070 us (0.86)
  waiting for transfers between devices: 930 us -> 725 us
  starting transfers between devices: 10.1 us -> 23.9 us
    all_gather x1 -> x0, waiting for transfers between devices: 200 us -> none  [body(): lax.all_gather(probe.astype(jnp.bfloat16), 'tile', axis=3, tiled=True)]
    psum x1, waiting for transfers between devices: 82.1 us -> 42.2 us  [body(): power = lax.psum(partial_power, 'mode')]
    ppermute x4, waiting for transfers between devices: 64.6 us -> 101 us  [from_behind(): return lax.ppermute(block, axis, route)]
    all_to_all x0 -> x1, starting transfers between devices: none -> 13.9 us  [body(): gathered = jnp.concatenate(lax.all_to_all(repeated, 'tile', 0, 0), axis=3)]
    unnamed x5 -> x4, waiting for transfers between devices: 532 us -> 532 us
  transfers between devices with their start and end apart: 8 -> 8, of which waited for: 8 -> 7; matrix products, arithmetic and copies ran while one was open for 3% -> 3% of each run, Pallas kernels for 0% -> 0%
where the time goes in v1:
time: 1070 us; the launch traced here: 1060 us
  waiting for transfers between devices  725 us (68%)
  blocking collectives  121 us (11%)
  matrix products  73.2 us (7%)
  local copies, waits for them, and re-layouts  65 us (6%)
  between operations  28.3 us (3%)
  starting transfers between devices  23.9 us (2%)
  other arithmetic  22.4 us (2%)
    unnamed x4, waiting for transfers between devices  532 us
    psum x1, blocking collectives, body(): lax.psum((object_sum, probe_sum), ('tile', 'mode'))  121 us
    ppermute x4, waiting for transfers between devices, from_behind(): return lax.ppermute(block, axis, route)  101 us
    psum x1, waiting for transfers between devices, body(): lax.psum(region_grad.astype(jnp.bfloat16), 'mode').astype(jnp.float32)  50.8 us
    psum x1, waiting for transfers between devices, body(): power = lax.psum(partial_power, 'mode')  42.2 us
    dot_general x24, matrix products, left_product(): jnp.einsum('ij,...jl->...il', table, right_data, preferred_element_type=j...  35.8 us
    dot_general x24, matrix products, right_product(): jnp.einsum('...jk,kl->...jl', left_data, table, preferred_element_type=jn...  30.7 us
    dynamic_update_slice x2, local copies, waits for them, and re-layouts, body(): lax.dynamic_update_slice(region_grad, current + slot_grads[slot_index], s...  23.4 us
  transfers between devices with their start and end apart: 8, of which 7 were waited for; matrix products, arithmetic and copies ran while one was open for 3% of the time, Pallas kernels for 0%

profile of v1, /device:TPU:1, one launch (start us, length us, event | category | flops | bytes accessed | tf_op | source)
XLA Modules:
  0.0 1058.7 jit_solution(7360482638565728733)
XLA Ops:
  8.1 3.3 stack.26
  11.4 13.9 %all-to-all-start = ((bf16[64,4,2,2,4,256]{5,3,4,2,1,0:T(2,128)(2,1)}), bf16[64,4,2,2,4,256]{5,3,4,2,1,0:T(2,128)(2,1)}, u32[]{:S(2)}, u32[]{:S(2)}) async-start(bf16[64,4,2,2,4,256]{5,3,4,2,1,0:T(2,128)(2,1)} %stack.26), calls=%async_computation | async-start | bytes 4194304 | tf_op jit(solution)/shard_map/all_to_all | solution.py:102
  26.7 23.5 %collective-permute-done = bf16[2,2,256,256]{3,2,1,0:T(8,128)(2,1)S(1)} collective-permute-done((bf16[2,2,256,256]{3,2,1,0:T(8,128)(2,1)S(1)}, bf16[2,2,256,256]{3,2,1,0:T(8,128)(2,1)S(1)}, u32[]{:S(2)}, u32[]{:S(2)}) %collective-permute-start) | collective-permute-done | bytes 524320 | tf_op jit(solution)/shard_map/ppermute | solution.py:16
  53.8 51.9 %collective-permute-done.1 = bf16[2,2,256,512]{3,2,1,0:T(8,128)(2,1)} collective-permute-done((bf16[2,2,256,512]{3,2,1,0:T(8,128)(2,1)S(1)}, bf16[2,2,256,512]{3,2,1,0:T(8,128)(2,1)}, u32[]{:S(2)}, u32[]{:S(2)}) %collective-permute-start.1) | collective-permute-done | bytes 1048608 | tf_op jit(solution)/shard_map/ppermute | solution.py:16
  107.1 6.0 while.1
  107.7 2.4 bitcast_dynamic-update-slice_fusion.2
  110.7 2.4 bitcast_dynamic-update-slice_fusion.2
  116.9 3.0 copy.139
  121.9 2.0 copy.141
  143.8 2.4 add_convert_fusion.2
  155.4 2.1 add_reduce_fusion.1
  163.2 2.1 copy.172
  168.4 42.2 %all-reduce.6.cloned.1.call-done = f32[2,256,256]{1,2,0:T(8,128)} async-done(((f32[2,256,256]{1,2,0:T(8,128)}), f32[2,256,256]{1,2,0:T(8,128)}) %all-reduce.6.cloned.1.call-update) | async-done | bytes 524304 | tf_op jit(solution)/shard_map/psum | solution.py:126
  221.2 2.5 add_reduce_fusion
  243.0 3.0 add_bitcast_fusion
  246.3 2.5 broadcast_in_dim.11
  248.8 11.2 %dynamic_update_slice.6 = f32[2,2,512,512]{2,3,1,0:T(8,128)} dynamic-update-slice(f32[2,2,512,512]{2,3,1,0:T(8,128)} %broadcast_in_dim.11, f32[2,2,256,256]{2,3,1,0:T(8,128)S(1)} %fusion.57, s32[]{:T(128)} %constant.27.clone.1, s32[]{:T(128)} %constant.27.clone.1, s32[]{:T(128)S(6)} %select_n.176, s32[]{:T(128)S(6)} %select_n.177) | dynamic-update-slice | bytes 2097156 | tf_op jit(solution)/shard_map/dynamic_update_slice | solution.py:153
  261.7 12.3 %dynamic_update_slice.7 = f32[2,2,512,512]{2,3,1,0:T(8,128)} dynamic-update-slice(f32[2,2,512,512]{2,3,1,0:T(8,128)} %dynamic_update_slice.6, f32[2,2,256,256]{2,3,1,0:T(8,128)S(1)} %fusion.59, s32[]{:T(128)} %constant.27.clone.1, s32[]{:T(128)} %constant.27.clone.1, s32[]{:T(128)S(6)} %select_n.178, s32[]{:T(128)S(6)} %select_n.179) | dynamic-update-slice | bytes 2097156 | tf_op jit(solution)/shard_map/dynamic_update_slice | solution.py:153
  274.0 3.9 convert_element_type.598
  281.0 3.1 copy.200
  284.1 6.6 fusion.156
  290.7 50.8 %all-reduce.8.cloned.1.call-done = bf16[2,2,512,512]{2,3,1,0:T(8,128)(2,1)} async-done(((bf16[2,2,512,512]{2,3,1,0:T(8,128)(2,1)}), bf16[2,2,512,512]{2,3,1,0:T(8,128)(2,1)}) %all-reduce.8.cloned.1.call-update) | async-done | bytes 2097168 | tf_op jit(solution)/shard_map/psum | solution.py:156
  343.0 3.4 collective-permute-start.2
  346.4 22.3 %collective-permute-done.2 = bf16[2,2,256,512]{2,3,1,0:T(8,128)(2,1)S(1)} collective-permute-done((bf16[2,2,256,512]{2,3,1,0:T(8,128)(2,1)S(1)}, bf16[2,2,256,512]{2,3,1,0:T(8,128)(2,1)S(1)}, u32[]{:S(2)}, u32[]{:S(2)}) %collective-permute-start.2) | collective-permute-done | bytes 1048608 | tf_op jit(solution)/shard_map/ppermute | solution.py:16
  369.7 3.9 collective-permute-start.3
  378.2 2.6 copy.198
  382.1 2.9 collective-permute-done.3
  385.0 1.9 multiply_reduce_fusion
  387.5 531.6 %all-reduce.10.cloned.1.call-done = f32[4,2,2,256,256]{4,0,3,2,1:T(4,128)} async-done(((f32[4,2,2,256,256]{4,0,3,2,1:T(4,128)}), f32[4,2,2,256,256]{4,0,3,2,1:T(4,128)}) %all-reduce.10.cloned.1.call-update) | async-done | bytes 4194320
  920.6 120.8 %all-reduce.1 = (f32[]{:T(128)}, f32[]{:T(128)}) all-reduce(f32[]{:T(128)S(6)} %div.27, f32[]{:T(128)} %multiply_reduce_fusion.1), channel_id=1, replica_groups=mesh['tile'=64,'mode'=4] {'tile','mode'}, use_global_device_ids=true, to_apply=%region_8.9 | all-reduce | flops 2 | bytes 16 | tf_op jit(solution)/shard_map/psum | solution.py:174
  1045.1 2.9 multiply_add_fusion
  1048.0 2.6 copy.203
  (153 shorter events, 88.4 us)
Async XLA Ops:
  11.4 14.0 %copy-start.10 = (f32[1,2,2,256,256]{4,3,2,1,0:T(8,128)S(1)}, f32[1,2,2,256,256]{4,3,2,1,0:T(8,128)}, u32[]{:S(2)}) copy-start(f32[1,2,2,256,256]{4,3,2,1,0:T(8,128)} %param.11) | copy-start | bytes 3145732
  11.4 15.3 %copy-start.22 = (s32[2,2]{1,0:T(2,128)S(1)}, s32[2,2]{1,0:T(2,128)}, u32[]{:S(2)}) copy-start(s32[2,2]{1,0:T(2,128)} %param.16) | copy-start | bytes 52
  11.4 105.5 %all-to-all-start = ((bf16[64,4,2,2,4,256]{5,3,4,2,1,0:T(2,128)(2,1)}), bf16[64,4,2,2,4,256]{5,3,4,2,1,0:T(2,128)(2,1)}, u32[]{:S(2)}, u32[]{:S(2)}) async-start(bf16[64,4,2,2,4,256]{5,3,4,2,1,0:T(2,128)(2,1)} %stack.26), calls=%async_computation | async-start | bytes 4194304 | tf_op jit(solution)/shard_map/all_to_all | solution.py:102
  25.3 26.5 %copy-start.24 = (s32[2]{0:T(128)S(1)}, s32[2]{0:T(128)}, u32[]{:S(2)}) copy-start(s32[2]{0:T(128)} %param.17) | copy-start | bytes 28
  25.3 185.3 %all-reduce.6.cloned.1.call-start = ((), (), s32[]{:S(2)}) async-start(), calls=%async_computation.1 | async-start | bytes 1048576 | tf_op jit(solution)/shard_map/psum | solution.py:126
  25.4 24.8 %collective-permute-start = (bf16[2,2,256,256]{3,2,1,0:T(8,128)(2,1)S(1)}, bf16[2,2,256,256]{3,2,1,0:T(8,128)(2,1)S(1)}, u32[]{:S(2)}, u32[]{:S(2)}) collective-permute-start(bf16[2,2,256,256]{3,2,1,0:T(8,128)(2,1)S(1)} %convert_bitcast_fusion), channel_id=1, source_target_pairs={{4,0},{8,4},{12,8},{16,12},{20,16},{24,20},{28,24},{32,28},{36,32}... | collective-permute-start | bytes 1572872 | tf_op jit(solution)/shard_map/ppermute | solution.py:16
  50.3 55.4 %collective-permute-start.1 = (bf16[2,2,256,512]{3,2,1,0:T(8,128)(2,1)S(1)}, bf16[2,2,256,512]{3,2,1,0:T(8,128)(2,1)}, u32[]{:S(2)}, u32[]{:S(2)}) collective-permute-start(bf16[2,2,256,512]{3,2,1,0:T(8,128)(2,1)S(1)} %pad_maximum_fusion.3), channel_id=1, source_target_pairs={{32,0},{36,4},{40,8},{44,12},{48,16},{52,20},{56,24},{60,28},{64,3... | collective-permute-start | bytes 3145736 | tf_op jit(solution)/shard_map/ppermute | solution.py:16
  114.6 9.4 copy-start.2
  114.9 9.2 copy-start.4
  124.1 1.6 copy-start
  130.8 2.5 copy-start.19
  141.2 2.5 copy-start.6
  141.2 2.5 copy-start.8
  157.5 184.0 %all-reduce.8.cloned.1.call-start = ((), (), s32[]{:S(2)}) async-start(), calls=%async_computation.2 | async-start | bytes 4194304 | tf_op jit(solution)/shard_map/psum | solution.py:156
  219.6 1.3 copy-start.7
  219.6 1.5 copy-start.12
  230.0 2.5 copy-start.18
  240.4 2.6 copy-start.1
  240.4 2.6 copy-start.3
  240.5 2.6 copy-start.5
  277.9 1.5 copy-start.14
  277.9 641.2 %all-reduce.10.cloned.1.call-start = ((), (), s32[]{:S(2)}) async-start(), calls=%async_computation.3 | async-start | bytes 8388608
  341.5 27.1 %copy-start.17 = (bf16[2,2,512,512]{2,3,1,0:T(8,128)(2,1)S(1)}, bf16[2,2,512,512]{2,3,1,0:T(8,128)(2,1)}, u32[]{:S(2)}) copy-start(bf16[2,2,512,512]{2,3,1,0:T(8,128)(2,1)} %all-reduce.8.cloned.1.call-done) | copy-start | bytes 6291460
  343.0 30.7 %copy-start.11 = (f32[1,2,2,256,256]{4,3,2,1,0:T(8,128)S(1)}, f32[1,2,2,256,256]{4,3,2,1,0:T(8,128)}, u32[]{:S(2)}) copy-start(f32[1,2,2,256,256]{4,3,2,1,0:T(8,128)} %param.11) | copy-start | bytes 3145732
  343.0 25.6 %collective-permute-start.2 = (bf16[2,2,256,512]{2,3,1,0:T(8,128)(2,1)S(1)}, bf16[2,2,256,512]{2,3,1,0:T(8,128)(2,1)S(1)}, u32[]{:S(2)}, u32[]{:S(2)}) collective-permute-start(bf16[2,2,256,512]{2,3,1,0:T(8,128)(2,1)S(1)} %slice.116), channel_id=1, source_target_pairs={{0,32},{4,36},{8,40},{12,44},{16,48},{20,52},{24,56},{28,60},{32,6... | collective-permute-start | bytes 3145736 | tf_op jit(solution)/shard_map/ppermute | solution.py:16
  368.8 6.8 copy-start.23
  369.7 15.3 %collective-permute-start.3 = (bf16[2,2,256,256]{2,3,1,0:T(8,128)(2,1)}, bf16[2,2,256,256]{2,3,1,0:T(8,128)(2,1)}, u32[]{:S(2)}, u32[]{:S(2)}) collective-permute-start(bf16[2,2,256,256]{2,3,1,0:T(8,128)(2,1)} %slice.159), channel_id=1, source_target_pairs={{0,4},{4,8},{8,12},{12,16},{16,20},{20,24},{24,28},{28,32},{32,36}... | collective-permute-start | bytes 1572872 | tf_op jit(solution)/shard_map/ppermute | solution.py:16
  373.7 7.2 copy-start.25
  375.0 667.1 %copy-start.20 = (f32[4,2,2,4,256]{4,3,2,1,0:T(4,128)S(1)}, f32[4,2,2,4,256]{4,3,2,1,0:T(4,128)}, u32[]{:S(2)}) copy-start(f32[4,2,2,4,256]{4,3,2,1,0:T(4,128)} %param.13) | copy-start | bytes 196612
  375.0 667.1 %copy-start.21 = (f32[4,2,2,4,256]{4,3,2,1,0:T(4,128)S(1)}, f32[4,2,2,4,256]{4,3,2,1,0:T(4,128)}, u32[]{:S(2)}) copy-start(f32[4,2,2,4,256]{4,3,2,1,0:T(4,128)} %param.14) | copy-start | bytes 196612
  378.2 666.9 %copy-start.15 = (f32[1,2,2,256,256]{3,4,2,1,0:T(8,128)S(1)}, f32[1,2,2,256,256]{3,4,2,1,0:T(8,128)}, u32[]{:S(2)}) copy-start(f32[1,2,2,256,256]{3,4,2,1,0:T(8,128)} %copy.199) | copy-start | bytes 3145732
  1048.0 2.6 copy-start.16
  (2 other events, 2.5 us)
Sparse Core Ops, SparseCore 0:
  157.7 52.8 all-reduce.5
  278.0 63.4 all-reduce.7
  344.2 574.9 all-reduce.9
